TPU v7x, 32 devices: a whole 2x2x4 slice. The times are simulated.
32 devices in a mesh: conv: 2 (over x), seq: 8 (over z, y), head: 2 (over core).
Axes of the slice: x: 2, y: 2, z: 4, core: 2. Of those that a mesh axis runs over, the one named last changes fastest.
Arguments:
- queries: bfloat16 [3072, 2048], P(('conv', 'seq'), 'head'), parts along dimension 0, may hold values from -10 to 10, as said below
- key_states: bfloat16 [3072, 512], P(('conv', 'seq'), 'head'), parts along dimension 0, may hold values from -5 to 5, as said below
- value_states: bfloat16 [3072, 512], P(('conv', 'seq'), 'head'), parts along dimension 0, may hold values from -16 to 16
- out_weight: bfloat16 [2048, 4096], P('head'), may hold values from -0.125 to 0.125
- turn_lengths: int32 [32], P('conv'), parts along dimension 0, may hold values from 1 to 959, as said below
- block_flags: int32 [16, 8], P(('conv', 'seq')), parts along dimension 0, may hold values 0 or 1
Outputs:
- pooled: float32 [32, 4096], P(('conv', 'seq'), 'head'), parts along dimension 0
There are 2 independent parts, one for each index of `conv`. A program takes and returns all parts, laid end to end along the dimension named above; an argument that names none is the same for every part. Nothing has to cross between parts.
Inputs may be any that keep to these rules, and one draw needn't show every extreme that they name: `queries`: every entry lies within the stated bounds. `key_states`: every entry lies within the stated bounds. `turn_lengths`: the lengths sum to 1536; turn 0 has one token and turn 1, the longest, has exactly 959 tokens.
All inputs are finite; a program needn't handle non-finite values. No bound on the sum of `block_flags` on one device may be relied on, other than what follows from the above.
Results may differ from a plain program's by a relative error of at most 0.0035.
Values may be sent and summed in bfloat16 or wider, within the bound.
A program may use at most 128 MiB of HBM per device.

v0:
```python
import math
import jax
import jax.numpy as jnp
from jax import lax
from jax.sharding import PartitionSpec as P

HD = 128
big_negative = -1e30
log_two_e = 1.4426950408889634


def on_device(queries, key_states, value_states, out_weight, turn_lengths, block_flags):
    q_rows = queries.shape[0]
    heads_here = queries.shape[1] // HD
    groups = key_states.shape[1] // HD
    repeat = heads_here // groups
    factor = log_two_e / math.sqrt(HD)
    my_index = lax.axis_index("seq")
    own_pos = my_index * q_rows + jnp.arange(q_rows, dtype=jnp.int32)
    block_count = block_flags.shape[1]
    row_pick = jnp.zeros((q_rows,), jnp.int32)
    query_block = own_pos // q_rows
    grouped = queries.reshape(q_rows, groups, repeat, HD)

    def mask_for(key_start, length):
        key_pos = key_start + jnp.arange(length, dtype=jnp.int32)
        key_block = key_pos // q_rows
        hits = key_block[:, None] == jnp.arange(block_count, dtype=jnp.int32)[None, :]
        allowed = jnp.sum(jnp.where(hits[None], block_flags[:, None, :], 0), axis=2)
        allowed_rows = jnp.where(row_pick[:, None] == 1, allowed[-1][None, :], allowed[0][None, :])
        causal = key_pos[None, :] <= own_pos[:, None]
        return causal & ((key_block[None, :] == query_block[:, None]) | (allowed_rows == 1))

    def attend(state, key_rows, value_rows, key_start):
        run_top, run_sum, totals = state
        length = key_rows.shape[0]
        visible = mask_for(key_start, length)[None, None]
        logit = (
            jnp.einsum(
                "qgrd,kgd->grqk",
                grouped,
                key_rows.reshape(length, groups, HD),
                preferred_element_type=jnp.float32,
            )
            * factor
        )
        logit = jnp.where(visible, logit, big_negative)
        new_top = jnp.maximum(run_top, jnp.ceil(jnp.max(logit, axis=-1)))
        weights = jnp.where(visible, jnp.exp2(logit - new_top[..., None]), 0.0)
        rescale = jnp.exp2(run_top - new_top)
        run_sum = run_sum * rescale + jnp.sum(weights, axis=-1)
        update = jnp.einsum(
            "grqk,kgd->grqd",
            weights.astype(jnp.bfloat16),
            value_rows.reshape(length, groups, HD),
            preferred_element_type=jnp.float32,
        )
        totals = totals * rescale[..., None] + update
        return (new_top, run_sum, totals)

    start_state = (
        jnp.full((groups, repeat, q_rows), big_negative, jnp.float32),
        jnp.zeros((groups, repeat, q_rows), jnp.float32),
        jnp.zeros((groups, repeat, q_rows, HD), jnp.float32),
    )
    key_piece = lax.all_gather(key_states, "seq", axis=0, tiled=True)
    value_piece = lax.all_gather(value_states, "seq", axis=0, tiled=True)
    length = key_piece.shape[0]
    width_step = math.gcd(length, 1024)

    def one_block(number, carried):
        offset = number * width_step
        key_rows = lax.dynamic_slice_in_dim(key_piece, offset, width_step, 0)
        value_rows = lax.dynamic_slice_in_dim(value_piece, offset, width_step, 0)
        return attend(carried, key_rows, value_rows, offset)

    run_top, run_sum, totals = lax.fori_loop(0, length // width_step, one_block, start_state)
    attended_work = (
        (totals / run_sum[..., None])
        .transpose(2, 0, 1, 3)
        .reshape(q_rows, heads_here * HD)
        .astype(jnp.bfloat16)
    )
    turn_ends = jnp.cumsum(turn_lengths)
    starts = turn_ends - turn_lengths
    member = (starts[:, None] <= own_pos[None, :]) & (own_pos[None, :] < turn_ends[:, None])
    turn_share = jnp.where(member, 1.0, 0.0).astype(jnp.float32) / turn_lengths[:, None].astype(
        jnp.float32
    )
    partial_rows = jnp.dot(attended_work, out_weight, preferred_element_type=jnp.float32)
    projected_rows = lax.psum_scatter(partial_rows, "head", scatter_dimension=1, tiled=True)
    pooled_part = jnp.dot(turn_share, projected_rows, precision=lax.Precision.HIGHEST)
    return lax.psum_scatter(pooled_part, "seq", scatter_dimension=0, tiled=True)


def solution(mesh):
    in_specs = (
        P(("conv", "seq"), "head"),
        P(("conv", "seq"), "head"),
        P(("conv", "seq"), "head"),
        P("head", None),
        P("conv"),
        P(("conv", "seq"), None),
    )
    out_specs = P(("conv", "seq"), "head")
    return jax.shard_map(
        on_device, mesh=mesh, in_specs=in_specs, out_specs=out_specs, check_vma=False
    )
```

profile of v0, /device:TPU:0, one launch (start us, length us, event | category | flops | bytes accessed | tf_op | source)
XLA Modules:
  0.0 211.3 jit_solution(6904133844643909026)
XLA Ops:
  6.5 36.3 %all_gather.6 = bf16[1536,256]{1,0:T(8,128)(2,1)} all-gather(bf16[192,256]{1,0:T(8,128)(2,1)} %param.9), channel_id=1, replica_groups=mesh['conv'=2,'seq'=8,'head'=2] {'seq'}, dimensions={0}, use_global_device_ids=true | all-gather | bytes 884736 | tf_op jit(solution)/shard_map/all_gather | solution.py:66
  42.9 34.2 %all_gather.7 = bf16[1536,256]{1,0:T(8,128)(2,1)} all-gather(bf16[192,256]{1,0:T(8,128)(2,1)} %param.10), channel_id=1, replica_groups=mesh['conv'=2,'seq'=8,'head'=2] {'seq'}, dimensions={0}, use_global_device_ids=true | all-gather | bytes 884736 | tf_op jit(solution)/shard_map/all_gather | solution.py:67
  77.1 1.3 reshape.229
  78.4 0.8 copy.26
  79.2 28.0 %while.22 = (s32[]{:T(128)}, f32[2,4,192]{2,1,0:T(4,128)S(1)}, f32[2,4,192]{2,1,0:T(4,128)S(1)}, f32[2,4,192,128]{3,2,1,0:T(8,128)}, s32[1,8]{1,0:T(1,128)S(1)},...) while((s32[]{:T(128)}, f32[2,4,192]{2,1,0:T(4,128)S(1)}, ...), condition=%wide.region_5.6_spmd.clone.clone.clone, body=%wide.region_1.5_spmd.clone.clone.clone.sunk | while | flops 415462080 | bytes 14534883 | solution.py:77
  79.5 1.1 constant_dynamic-slice_fusion.4
  80.6 0.8 copy.39
  81.4 1.8 fusion.54
  83.3 1.2 fusion.55
  84.5 0.8 copy.40
  85.3 3.1 %fusion.57 = f32[2,4,192,128]{3,2,1,0:T(8,128)} fusion(bf16[512,2,128,1]{0,2,3,1:T(8,128)(2,1)} %bitcast.53, f32[2,512,192,4]{1,2,3,0:T(8,128)S(1)} %get-tuple-element.465, f32[2,4,192]{2,1,0:T(4,128)S(1)} %ceil_maximum_fusion.2, pred[192,512]{1,0:T(8,128)(4,1)S(1)} %or_and_fusion.2, f32[2,4,192,128]{3,2,1,0:T(8,128)} %get-tuple-element.485, ...), kind=kOutput, calls=%fused_computation.9.clone.1 | convolution fusion | flops 206635008 | bytes 5091329 | tf_op jit(solution)/shard_map/while/body/eval_jaxpr/grqk,kgd->grqd/dot_general | solution.py:52
  88.8 1.1 constant_dynamic-slice_fusion.4
  89.8 0.8 copy.39
  90.7 1.8 fusion.54
  92.5 1.2 fusion.55
  93.8 0.8 copy.40
  94.6 3.2 %fusion.57 = f32[2,4,192,128]{3,2,1,0:T(8,128)} fusion(bf16[512,2,128,1]{0,2,3,1:T(8,128)(2,1)} %bitcast.53, f32[2,512,192,4]{1,2,3,0:T(8,128)S(1)} %get-tuple-element.465, f32[2,4,192]{2,1,0:T(4,128)S(1)} %ceil_maximum_fusion.2, pred[192,512]{1,0:T(8,128)(4,1)S(1)} %or_and_fusion.2, f32[2,4,192,128]{3,2,1,0:T(8,128)} %get-tuple-element.485, ...), kind=kOutput, calls=%fused_computation.9.clone.1 | convolution fusion | flops 206635008 | bytes 5091329 | tf_op jit(solution)/shard_map/while/body/eval_jaxpr/grqk,kgd->grqd/dot_general | solution.py:52
  98.1 1.1 constant_dynamic-slice_fusion.4
  99.2 0.8 copy.39
  100.1 1.8 fusion.54
  101.9 1.2 fusion.55
  103.1 0.8 copy.40
  104.0 3.2 %fusion.57 = f32[2,4,192,128]{3,2,1,0:T(8,128)} fusion(bf16[512,2,128,1]{0,2,3,1:T(8,128)(2,1)} %bitcast.53, f32[2,512,192,4]{1,2,3,0:T(8,128)S(1)} %get-tuple-element.465, f32[2,4,192]{2,1,0:T(4,128)S(1)} %ceil_maximum_fusion.2, pred[192,512]{1,0:T(8,128)(4,1)S(1)} %or_and_fusion.2, f32[2,4,192,128]{3,2,1,0:T(8,128)} %get-tuple-element.485, ...), kind=kOutput, calls=%fused_computation.9.clone.1 | convolution fusion | flops 206635008 | bytes 5091329 | tf_op jit(solution)/shard_map/while/body/eval_jaxpr/grqk,kgd->grqd/dot_general | solution.py:52
  107.2 1.4 fusion.19
  108.6 0.3 copy.28
  109.2 6.9 %fusion.35 = f32[192,4096]{1,0:T(8,128)} fusion(bf16[192,1024]{1,0:T(8,128)(2,1)S(1)} %convert_element_type.26, bf16[1024,4096]{1,0:T(8,128)(2,1)} %param.11), kind=kOutput, calls=%fused_computation.51 | convolution fusion | flops 1610612736 | bytes 11927552 | tf_op jit(solution)/shard_map/dot_general | solution.py:90
  116.1 0.6 copy-done.1
  117.0 11.5 %reduce-scatter.2.cloned.1.call-done = f32[192,2048]{1,0:T(8,128)} async-done(((f32[192,4096]{1,0:T(8,128)}), f32[192,2048]{1,0:T(8,128)}) %reduce-scatter.2.cloned.1.call-update) | async-done | bytes 1572880 | tf_op jit(solution)/shard_map/reduce_scatter | solution.py:91
  128.5 2.9 %fusion.20 = f32[16,2048]{1,0:T(8,128)} fusion(f32[192,2048]{1,0:T(8,128)} %reduce-scatter.2.cloned.1.call-done, f32[16]{0:T(128)S(1)} %get-tuple-element.393, s32[192]{0:T(256)S(1)} %iota_add_fusion.2, s32[16]{0:T(128)S(1)} %reduce.6, s32[16]{0:T(128)S(1)} %get-tuple-element.392), kind=kOutput, calls=%fused_computation.34 | convolution fusion | flops 75512832 | bytes 1704896 | tf_op jit(solution)/shard_map/dot_general | solution.py:92
  131.4 0.6 dynamic-slice
  132.6 70.4 %all-reduce.3.cloned.1.call-done = f32[16,2048]{1,0:T(8,128)} async-done(((f32[16,2048]{1,0:T(8,128)}), f32[16,2048]{1,0:T(8,128)}) %all-reduce.3.cloned.1.call-update) | async-done | bytes 131088
  203.0 1.5 constant_dynamic-slice_fusion.2
  (42 shorter events, 1.6 us)
Async XLA Ops:
  6.5 72.6 %copy-start = (s32[1,8]{1,0:T(1,128)S(1)}, s32[1,8]{1,0:T(1,128)}, u32[]{:S(2)}) copy-start(s32[1,8]{1,0:T(1,128)} %param.13) | copy-start | bytes 100
  6.5 121.9 %reduce-scatter.2.cloned.1.call-start = ((), (), s32[]{:S(2)}) async-start(), calls=%async_computation.1 | async-start | bytes 4718592 | tf_op jit(solution)/shard_map/reduce_scatter | solution.py:91
  116.1 0.7 copy-start.1
  116.1 15.3 %copy-start.2 = (u32[32]{0:T(128)S(1)}, u32[32]{0:T(128)}, u32[]{:S(2)}) copy-start(u32[32]{0:T(128)} %constant.141) | copy-start | bytes 388
  116.1 86.9 %all-reduce.3.cloned.1.call-start = ((), (), s32[]{:S(2)}) async-start(), calls=%async_computation.2 | async-start | bytes 262144
Sparse Core Ops, SparseCore 0:
  116.2 12.2 reduce-scatter.1
  132.2 70.7 all-reduce.2
where the time goes:
time: 212 us; the launch traced here: 211 us
  waiting for transfers between devices  81.9 us (39%)
  blocking collectives  70.6 us (33%)
  matrix products  24.8 us (12%)
  between operations  14.1 us (7%)
  local copies, waits for them, and re-layouts  13.6 us (6%)
  other arithmetic  6.13 us (3%)
    unnamed x3, waiting for transfers between devices  70.4 us
    all_gather x1, blocking collectives, on_device(): key_piece = lax.all_gather(key_states, 'seq', axis=0, tiled=True)  36.3 us
    all_gather x1, blocking collectives, on_device(): value_piece = lax.all_gather(value_states, 'seq', axis=0, tiled=True)  34.2 us
    reduce_scatter x1, waiting for transfers between devices, on_device(): lax.psum_scatter(partial_rows, 'head', scatter_dimension=1, tiled=True)  11.5 us
    dot_general x3, matrix products, attend(): jnp.einsum('grqk,kgd->grqd', weights.astype(jnp.bfloat16), value_rows.res...  9.53 us
    dot_general x1, matrix products, on_device(): jnp.dot(attended_work, out_weight, preferred_element_type=jnp.float32)  6.85 us
    dynamic_slice x6, local copies, waits for them, and re-layouts, one_block(): value_rows = lax.dynamic_slice_in_dim(value_piece, offset, width_step, 0)  5.76 us
    dot_general x3, matrix products, attend(): jnp.einsum('qgrd,kgd->grqk', grouped, key_rows.reshape(length, groups, HD...  5.5 us
  transfers between devices with their start and end apart: 2, of which 2 were waited for; matrix products, arithmetic and copies ran while one was open for 0% of the time, Pallas kernels for 0%

commit v1 on v0

--- a/solution.py
+++ b/solution.py
@@ -63,8 +63,13 @@
         jnp.zeros((groups, repeat, q_rows), jnp.float32),
         jnp.zeros((groups, repeat, q_rows, HD), jnp.float32),
     )
-    key_piece = lax.all_gather(key_states, "seq", axis=0, tiled=True)
-    value_piece = lax.all_gather(value_states, "seq", axis=0, tiled=True)
+    key_piece, value_piece = jnp.split(
+        lax.all_gather(
+            jnp.concatenate([key_states, value_states], axis=1), "seq", axis=0, tiled=True
+        ),
+        [key_states.shape[1]],
+        axis=1,
+    )
     length = key_piece.shape[0]
     width_step = math.gcd(length, 1024)
 

time: 212 us -> 189 us (0.89)
  blocking collectives: 70.6 us -> 0 us
  waiting for transfers between devices: 81.9 us -> 125 us
  local copies, waits for them, and re-layouts: 13.6 us -> 16.2 us
    all_gather x2 -> x0, blocking collectives: 70.6 us -> none  [the longest x1 36.3 us: on_device(): key_piece = lax.all_gather(key_states, 'seq', axis=0, tiled=True)]
    all_gather x0 -> x1, waiting for transfers between devices: none -> 46.1 us  [on_device(): lax.all_gather(jnp.concatenate([key_states, value_states], axis=1), 'seq'...]
    split x0 -> x1, local copies, waits for them, and re-layouts: none -> 2.62 us  [on_device(): jnp.split(lax.all_gather(jnp.concatenate([key_states, value_states], axis...]
    reduce_scatter x1, waiting for transfers between devices: 11.5 us -> 8.99 us  [on_device(): lax.psum_scatter(partial_rows, 'head', scatter_dimension=1, tiled=True)]
    unnamed x3 -> x4, waiting for transfers between devices: 70.4 us -> 70.4 us
  transfers between devices with their start and end apart: 2 -> 3, of which waited for: 2 -> 3; matrix products, arithmetic and copies ran while one was open for 0% -> 2% of each run, Pallas kernels for 0% -> 0%
where the time goes in v1:
time: 189 us; the launch traced here: 188 us
  waiting for transfers between devices  125 us (66%)
  matrix products  24.8 us (13%)
  local copies, waits for them, and re-layouts  16.2 us (9%)
  between operations  13.8 us (7%)
  other arithmetic  7.76 us (4%)
    unnamed x4, waiting for transfers between devices  70.4 us
    all_gather x1, waiting for transfers between devices, on_device(): lax.all_gather(jnp.concatenate([key_states, value_states], axis=1), 'seq'...  46.1 us
    dot_general x3, matrix products, attend(): jnp.einsum('grqk,kgd->grqd', weights.astype(jnp.bfloat16), value_rows.res...  9.55 us
    reduce_scatter x1, waiting for transfers between devices, on_device(): lax.psum_scatter(partial_rows, 'head', scatter_dimension=1, tiled=True)  8.99 us
    dot_general x1, matrix products, on_device(): jnp.dot(attended_work, out_weight, preferred_element_type=jnp.float32)  6.85 us
    dynamic_slice x6, local copies, waits for them, and re-layouts, one_block(): value_rows = lax.dynamic_slice_in_dim(value_piece, offset, width_step, 0)  5.72 us
    dot_general x3, matrix products, attend(): jnp.einsum('qgrd,kgd->grqk', grouped, key_rows.reshape(length, groups, HD...  5.5 us
  transfers between devices with their start and end apart: 3, of which 3 were waited for; matrix products, arithmetic and copies ran while one was open for 2% of the time, Pallas kernels for 0%

profile of v1, /device:TPU:0, one launch (start us, length us, event | category | flops | bytes accessed | tf_op | source)
XLA Modules:
  0.0 188.3 jit_solution(15696550019272096463)
XLA Ops:
  6.5 1.6 pad_maximum_fusion
  8.3 1.3 reshape.229
  9.5 0.8 copy.26
  10.3 46.1 %all-gather.2.cloned.1.call-done = bf16[1536,512]{1,0:T(8,128)(2,1)} async-done(((bf16[192,512]{1,0:T(8,128)(2,1)}), bf16[1536,512]{1,0:T(8,128)(2,1)}) %all-gather.2.cloned.1.call-update) | async-done | bytes 1572880 | tf_op jit(solution)/shard_map/all_gather | solution.py:67
  56.5 2.6 %fusion.34 = (bf16[1536,256]{1,0:T(8,128)(2,1)}, bf16[1536,256]{1,0:T(8,128)(2,1)}) fusion(bf16[1536,512]{1,0:T(8,128)(2,1)} %all-gather.2.cloned.1.call-done), kind=kLoop, calls=%fused_computation.51 | loop fusion | bytes 3145728 | tf_op jit(solution)/shard_map/split | solution.py:66
  59.1 28.0 %while.22 = (s32[]{:T(128)}, f32[2,4,192]{2,1,0:T(4,128)S(1)}, f32[2,4,192]{2,1,0:T(4,128)S(1)}, f32[2,4,192,128]{3,2,1,0:T(8,128)}, s32[1,8]{1,0:T(1,128)S(1)},...) while((s32[]{:T(128)}, f32[2,4,192]{2,1,0:T(4,128)S(1)}, ...), condition=%wide.region_5.6_spmd.clone.clone.clone, body=%wide.region_1.5_spmd.clone.clone.clone.sunk | while | flops 415462080 | bytes 14534883 | solution.py:82
  59.4 1.1 constant_dynamic-slice_fusion.4
  60.5 0.8 copy.39
  61.3 1.8 fusion.55
  63.2 1.2 fusion.56
  64.4 0.8 copy.40
  65.2 3.1 %fusion.58 = f32[2,4,192,128]{3,2,1,0:T(8,128)} fusion(bf16[512,2,128,1]{0,2,3,1:T(8,128)(2,1)} %bitcast.53, f32[2,512,192,4]{1,2,3,0:T(8,128)S(1)} %get-tuple-element.467, f32[2,4,192]{2,1,0:T(4,128)S(1)} %ceil_maximum_fusion.2, pred[192,512]{1,0:T(8,128)(4,1)S(1)} %or_and_fusion.2, f32[2,4,192,128]{3,2,1,0:T(8,128)} %get-tuple-element.487, ...), kind=kOutput, calls=%fused_computation.9.clone.1 | convolution fusion | flops 206635008 | bytes 5091329 | tf_op jit(solution)/shard_map/while/body/eval_jaxpr/grqk,kgd->grqd/dot_general | solution.py:52
  68.6 1.1 constant_dynamic-slice_fusion.4
  69.7 0.8 copy.39
  70.5 1.8 fusion.55
  72.4 1.2 fusion.56
  73.6 0.8 copy.40
  74.5 3.2 %fusion.58 = f32[2,4,192,128]{3,2,1,0:T(8,128)} fusion(bf16[512,2,128,1]{0,2,3,1:T(8,128)(2,1)} %bitcast.53, f32[2,512,192,4]{1,2,3,0:T(8,128)S(1)} %get-tuple-element.467, f32[2,4,192]{2,1,0:T(4,128)S(1)} %ceil_maximum_fusion.2, pred[192,512]{1,0:T(8,128)(4,1)S(1)} %or_and_fusion.2, f32[2,4,192,128]{3,2,1,0:T(8,128)} %get-tuple-element.487, ...), kind=kOutput, calls=%fused_computation.9.clone.1 | convolution fusion | flops 206635008 | bytes 5091329 | tf_op jit(solution)/shard_map/while/body/eval_jaxpr/grqk,kgd->grqd/dot_general | solution.py:52
  78.0 1.1 constant_dynamic-slice_fusion.4
  79.1 0.8 copy.39
  79.9 1.8 fusion.55
  81.8 1.2 fusion.56
  83.0 0.8 copy.40
  83.8 3.2 %fusion.58 = f32[2,4,192,128]{3,2,1,0:T(8,128)} fusion(bf16[512,2,128,1]{0,2,3,1:T(8,128)(2,1)} %bitcast.53, f32[2,512,192,4]{1,2,3,0:T(8,128)S(1)} %get-tuple-element.467, f32[2,4,192]{2,1,0:T(4,128)S(1)} %ceil_maximum_fusion.2, pred[192,512]{1,0:T(8,128)(4,1)S(1)} %or_and_fusion.2, f32[2,4,192,128]{3,2,1,0:T(8,128)} %get-tuple-element.487, ...), kind=kOutput, calls=%fused_computation.9.clone.1 | convolution fusion | flops 206635008 | bytes 5091329 | tf_op jit(solution)/shard_map/while/body/eval_jaxpr/grqk,kgd->grqd/dot_general | solution.py:52
  87.1 1.4 fusion.19
  89.1 6.9 %fusion.36 = f32[192,4096]{1,0:T(8,128)} fusion(bf16[192,1024]{1,0:T(8,128)(2,1)S(1)} %convert_element_type.26, bf16[1024,4096]{1,0:T(8,128)(2,1)} %param.11), kind=kOutput, calls=%fused_computation.53 | convolution fusion | flops 1610612736 | bytes 11927552 | tf_op jit(solution)/shard_map/dot_general | solution.py:95
  96.0 0.6 copy-done.1
  96.8 9.0 %reduce-scatter.2.cloned.1.call-done = f32[192,2048]{1,0:T(8,128)} async-done(((f32[192,4096]{1,0:T(8,128)}), f32[192,2048]{1,0:T(8,128)}) %reduce-scatter.2.cloned.1.call-update) | async-done | bytes 1572880 | tf_op jit(solution)/shard_map/reduce_scatter | solution.py:96
  105.8 2.9 %fusion.20 = f32[16,2048]{1,0:T(8,128)} fusion(f32[192,2048]{1,0:T(8,128)} %reduce-scatter.2.cloned.1.call-done, f32[16]{0:T(128)S(1)} %get-tuple-element.395, s32[192]{0:T(256)S(1)} %iota_add_fusion.2, s32[16]{0:T(128)S(1)} %reduce.6, s32[16]{0:T(128)S(1)} %get-tuple-element.394), kind=kOutput, calls=%fused_computation.35 | convolution fusion | flops 75512832 | bytes 1704896 | tf_op jit(solution)/shard_map/dot_general | solution.py:97
  108.8 0.6 dynamic-slice
  110.0 70.3 %all-reduce.3.cloned.1.call-done = f32[16,2048]{1,0:T(8,128)} async-done(((f32[16,2048]{1,0:T(8,128)}), f32[16,2048]{1,0:T(8,128)}) %all-reduce.3.cloned.1.call-update) | async-done | bytes 131088
  180.3 1.5 constant_dynamic-slice_fusion.2
  (45 shorter events, 1.9 us)
Async XLA Ops:
  6.5 52.5 %copy-start = (s32[1,8]{1,0:T(1,128)S(1)}, s32[1,8]{1,0:T(1,128)}, u32[]{:S(2)}) copy-start(s32[1,8]{1,0:T(1,128)} %param.13) | copy-start | bytes 100
  6.5 49.9 %all-gather.2.cloned.1.call-start = ((), (), s32[]{:S(2)}) async-start(), calls=%async_computation.1 | async-start | bytes 1769472 | tf_op jit(solution)/shard_map/all_gather | solution.py:67
  8.2 97.6 %reduce-scatter.2.cloned.1.call-start = ((), (), s32[]{:S(2)}) async-start(), calls=%async_computation.2 | async-start | bytes 4718592 | tf_op jit(solution)/shard_map/reduce_scatter | solution.py:96
  95.9 0.7 copy-start.1
  95.9 12.8 %copy-start.2 = (u32[32]{0:T(128)S(1)}, u32[32]{0:T(128)}, u32[]{:S(2)}) copy-start(u32[32]{0:T(128)} %constant.141) | copy-start | bytes 388
  95.9 84.4 %all-reduce.3.cloned.1.call-start = ((), (), s32[]{:S(2)}) async-start(), calls=%async_computation.3 | async-start | bytes 262144
Sparse Core Ops, SparseCore 0:
  9.5 46.8 all-gather.1
  96.1 9.7 reduce-scatter.1
  109.5 70.7 all-reduce.2
